TPU v7x, 128 devices: a whole 4x4x4 slice. The times are simulated.
128 devices in a mesh: freq: 2 (over core), vs: 64 (over z, y, x).
Axes of the slice: x: 4, y: 4, z: 4, core: 2. Of those that a mesh axis runs over, the one named last changes fastest.
Arguments:
- kernel: bfloat16 [4, 2, 256, 16384], P('freq', None, None, 'vs'), may hold values from -0.03125 to 0.03125
- sources: bfloat16 [4, 2, 2048, 16384], P('freq', None, 'vs'), may hold values from -6 to 6
- observed: float32 [256, 160, 2048], P('freq', None, 'vs'), may hold values from -6 to 6
- gate_start: int32 [256], P('freq'), may hold values from 0 to 80, as said below
- gate_length: int32 [256], P('freq'), may hold values from 1 to 160
Outputs:
- gradient: bfloat16 [4, 2, 2048, 16384], P('freq', None, 'vs')
- misfit: float32 [256, 160, 2048], P('freq', None, 'vs')
Inputs may be any that keep to these rules, and one draw needn't show every extreme that they name: gate_start + gate_length <= 160 for every receiver.
All inputs are finite; a program needn't handle non-finite values.
Results may differ from a plain program's by a relative error of at most 0.0057.
Values may be sent and summed in bfloat16 or wider, within the bound.
No kernel may reach another device: no remote copies, remote signals or barrier semaphores. Data moves between devices by JAX's collectives and lax.ppermute only.
A program may use at most 128 MiB of HBM per device.

v0:
```python
import jax
import jax.numpy as jnp
from jax import lax
from jax.sharding import PartitionSpec as P

NS = 16384
RW = 256


def complex_apply(kern, model):
    form = "frs,fvs->frv"
    real_part = jnp.einsum(
        form, kern[:, 0], model[:, 0], preferred_element_type=jnp.float32
    ) - jnp.einsum(form, kern[:, 1], model[:, 1], preferred_element_type=jnp.float32)
    imag_part = jnp.einsum(
        form, kern[:, 0], model[:, 1], preferred_element_type=jnp.float32
    ) + jnp.einsum(form, kern[:, 1], model[:, 0], preferred_element_type=jnp.float32)
    return jnp.stack([real_part, imag_part], 1)


def complex_adjoint(kern, spectrum):
    form = "frv,frs->fvs"
    real_part = jnp.einsum(
        form, spectrum[:, 0], kern[:, 0], preferred_element_type=jnp.float32
    ) + jnp.einsum(form, spectrum[:, 1], kern[:, 1], preferred_element_type=jnp.float32)
    imag_part = jnp.einsum(
        form, spectrum[:, 1], kern[:, 0], preferred_element_type=jnp.float32
    ) - jnp.einsum(form, spectrum[:, 0], kern[:, 1], preferred_element_type=jnp.float32)
    factor = (NS / RW) ** 0.5
    return factor * jnp.stack([real_part, imag_part], 1)


def transform_tables(count, samples):
    sample_index = jnp.arange(samples, dtype=jnp.int32)
    bin_index = samples // 4 + jnp.arange(count, dtype=jnp.int32)
    phase = sample_index[:, None] * bin_index[None, :] % samples
    theta = 2.0 * jnp.pi / samples * phase.astype(jnp.float32)
    return (jnp.cos(theta), jnp.sin(theta))


def local(kernel, sources, observed, gate_start, gate_length):
    gathered = lax.all_gather(kernel, "vs", axis=3, tiled=True)
    forward = complex_apply(gathered, sources)
    field = forward.astype(jnp.bfloat16)
    timed = lax.all_to_all(field, "freq", split_axis=2, concat_axis=0, tiled=True)
    count = timed.shape[0]
    samples = observed.shape[1]
    cosine, sine = transform_tables(count, samples)
    scale = count ** (-0.5)
    values = timed.astype(jnp.float32)
    highest = lax.Precision.HIGHEST
    signal = scale * (
        jnp.einsum("tf,frv->rtv", cosine, values[:, 0], precision=highest)
        - jnp.einsum("tf,frv->rtv", sine, values[:, 1], precision=highest)
    )
    sample_index = jnp.arange(samples, dtype=jnp.int32)
    inside = (sample_index[None, :] >= gate_start[:, None]) & (
        sample_index[None, :] < (gate_start + gate_length)[:, None]
    )
    gate_mask = inside.astype(jnp.float32)
    misfit = gate_mask[:, :, None] * (signal - observed)
    back_real = scale * jnp.einsum("tf,rtv->frv", cosine, misfit, precision=highest)
    back_imag = -scale * jnp.einsum("tf,rtv->frv", sine, misfit, precision=highest)
    back_spectrum = jnp.stack([back_real, back_imag], 1).astype(jnp.bfloat16)
    spectral = lax.all_to_all(back_spectrum, "freq", split_axis=0, concat_axis=2, tiled=True)
    gradient = complex_adjoint(gathered, spectral).astype(jnp.bfloat16)
    return (gradient, misfit)


def solution(mesh):
    return jax.shard_map(
        local,
        mesh=mesh,
        in_specs=(
            P("freq", None, None, "vs"),
            P("freq", None, "vs", None),
            P("freq", None, "vs"),
            P("freq"),
            P("freq"),
        ),
        out_specs=(P("freq", None, "vs", None), P("freq", None, "vs")),
        check_vma=False,
    )
```

profile of v0, /device:TPU:1, one launch (start us, length us, event | category | flops | bytes accessed | tf_op | source)
XLA Modules:
  0.0 335.3 jit_solution(14792505252984407137)
XLA Ops:
  7.2 0.0 all-gather.2.cloned.1.call-start
  7.2 1.9 copy.15
  9.1 0.0 all-gather.2.cloned.1.call-update
  9.1 0.7 add.36
  9.8 0.7 fusion.41
  10.5 229.3 %all-gather.2.cloned.1.call-done = bf16[2,2,256,16384]{3,2,0,1:T(8,128)(2,1)} async-done(((bf16[2,2,256,256]{3,2,0,1:T(8,128)(2,1)}), bf16[2,2,256,16384]{3,2,0,1:T(8,128)(2,1)}) %all-gather.2.cloned.1.call-update) | async-done | bytes 33554448 | tf_op jit(solution)/shard_map/all_gather | solution.py:42
  239.8 0.0 copy-start.1
  239.8 10.0 %fusion.4 = f32[2,256,32]{1,2,0:T(8,128)S(1)} fusion(bf16[2,2,256,16384]{3,2,0,1:T(8,128)(2,1)} %all-gather.2.cloned.1.call-done, bf16[2,2,32,16384]{3,2,1,0:T(8,128)(2,1)} %param.6), kind=kOutput, calls=%fused_computation.8 | convolution fusion | flops 536870912 | bytes 18939904 | tf_op jit(solution)/shard_map/frs,fvs->frv/dot_general | solution.py:15
  249.7 0.0 copy-done.1
  249.7 8.6 %fusion.5 = f32[2,256,32]{1,2,0:T(8,128)S(1)} fusion(bf16[2,2,256,16384]{3,2,0,1:T(8,128)(2,1)} %all-gather.2.cloned.1.call-done, bf16[2,2,32,16384]{3,2,1,0:T(8,128)(2,1)S(1)} %copy-done.1), kind=kOutput, calls=%fused_computation.9 | convolution fusion | flops 536870912 | bytes 18939904 | tf_op jit(solution)/shard_map/frs,fvs->frv/dot_general | solution.py:12
  258.4 8.6 %fusion.37 = bf16[2,1,256,32]{2,3,0,1:T(8,128)(2,1)S(1)} fusion(f32[2,256,32]{1,2,0:T(8,128)S(1)} %fusion.4, bf16[2,2,32,16384]{3,2,1,0:T(8,128)(2,1)S(1)} %copy-done.1, bf16[2,2,256,16384]{3,2,0,1:T(8,128)(2,1)} %all-gather.2.cloned.1.call-done), kind=kOutput, calls=%fused_computation.35 | convolution fusion | flops 536903680 | bytes 18972672 | tf_op jit(solution)/shard_map/frs,fvs->frv/dot_general | solution.py:17
  267.0 8.6 %fusion.34 = bf16[2,1,256,32]{2,3,0,1:T(8,128)(2,1)S(1)} fusion(f32[2,256,32]{1,2,0:T(8,128)S(1)} %fusion.5, bf16[2,2,32,16384]{3,2,1,0:T(8,128)(2,1)S(1)} %copy-done.1, bf16[2,2,256,16384]{3,2,0,1:T(8,128)(2,1)} %all-gather.2.cloned.1.call-done), kind=kOutput, calls=%fused_computation.34 | convolution fusion | flops 536903680 | bytes 18972672 | tf_op jit(solution)/shard_map/frs,fvs->frv/dot_general | solution.py:14
  275.7 0.0 copy-start
  275.7 0.2 copy.18
  275.9 0.3 reshape.54
  276.2 5.6 %all_to_all.36 = bf16[2,2,8192]{2,1,0:T(2,128)(2,1)S(1)} all-to-all(bf16[2,2,8192]{2,1,0:T(2,128)(2,1)S(1)} %reshape.54), channel_id=1, replica_groups=mesh['freq'=2,'vs'=64] {'freq'}, dimensions={0} | all-to-all | bytes 131072 | tf_op jit(solution)/shard_map/all_to_all | solution.py:45
  281.8 0.2 reshape.55
  282.0 0.1 copy.19
  282.1 1.3 fusion.42
  283.5 0.0 copy-done
  283.5 3.0 fusion.9
  286.5 1.4 fusion.32
  287.9 1.4 fusion.33
  289.3 3.0 copy.24
  292.4 3.8 %all_to_all.37 = bf16[4,2,128,32]{2,3,1,0:T(8,128)(2,1)S(1)} all-to-all(bf16[4,2,128,32]{2,3,1,0:T(8,128)(2,1)S(1)} %copy.21), channel_id=1, replica_groups=mesh['freq'=2,'vs'=64] {'freq'}, dimensions={0} | all-to-all | bytes 131072 | tf_op jit(solution)/shard_map/all_to_all | solution.py:65
  296.2 0.1 copy.29
  296.4 7.3 %fusion.2 = f32[2,32,16384]{2,1,0:T(8,128)S(1)} fusion(bf16[2,2,256,16384]{3,2,0,1:T(8,128)(2,1)} %all-gather.2.cloned.1.call-done, bf16[2,2,256,32]{2,3,0,1:T(8,128)(2,1)S(1)} %all_to_all.33), kind=kOutput, calls=%fused_computation.6 | convolution fusion | flops 536870912 | bytes 21004288 | tf_op jit(solution)/shard_map/frv,frs->fvs/dot_general | solution.py:26
  303.7 7.3 %fusion.3 = f32[2,32,16384]{2,1,0:T(8,128)S(1)} fusion(bf16[2,2,256,16384]{3,2,0,1:T(8,128)(2,1)} %all-gather.2.cloned.1.call-done, bf16[2,2,256,32]{2,3,0,1:T(8,128)(2,1)S(1)} %all_to_all.33), kind=kOutput, calls=%fused_computation.7 | convolution fusion | flops 536870912 | bytes 21004288 | tf_op jit(solution)/shard_map/frv,frs->fvs/dot_general | solution.py:23
  311.0 7.3 %fusion.1 = f32[2,1,32,16384]{3,2,0,1:T(8,128)S(1)} fusion(f32[2,32,16384]{2,1,0:T(8,128)S(1)} %fusion.2, bf16[2,2,256,16384]{3,2,0,1:T(8,128)(2,1)} %all-gather.2.cloned.1.call-done, bf16[2,2,256,32]{2,3,0,1:T(8,128)(2,1)S(1)} %all_to_all.33), kind=kOutput, calls=%fused_computation.3 | convolution fusion | flops 537919488 | bytes 25198592 | tf_op jit(solution)/shard_map/frv,frs->fvs/dot_general | solution.py:28
  318.3 7.3 %fusion = f32[2,1,32,16384]{3,2,0,1:T(8,128)S(1)} fusion(f32[2,32,16384]{2,1,0:T(8,128)S(1)} %fusion.3, bf16[2,2,256,16384]{3,2,0,1:T(8,128)(2,1)} %all-gather.2.cloned.1.call-done, bf16[2,2,256,32]{2,3,0,1:T(8,128)(2,1)S(1)} %all_to_all.33), kind=kOutput, calls=%fused_computation.2 | convolution fusion | flops 537919488 | bytes 25198592 | tf_op jit(solution)/shard_map/frv,frs->fvs/dot_general | solution.py:25
  325.7 0.5 fusion.8
  326.2 2.3 copy.23
  (5 shorter events, 0.1 us)
Async XLA Ops:
  7.2 232.6 %all-gather.2.cloned.1.call-start = ((), (), s32[]{:S(2)}) async-start(), calls=%async_computation.2 | async-start | bytes 34078720 | tf_op jit(solution)/shard_map/all_gather | solution.py:42
  239.8 10.0 %copy-start.1 = (bf16[2,2,32,16384]{3,2,1,0:T(8,128)(2,1)S(1)}, bf16[2,2,32,16384]{3,2,1,0:T(8,128)(2,1)}, u32[]{:S(2)}) copy-start(bf16[2,2,32,16384]{3,2,1,0:T(8,128)(2,1)} %param.6) | copy-start | bytes 12582916
  275.7 7.8 %copy-start = (f32[128,160,32]{0,2,1:T(8,128)S(1)}, f32[128,160,32]{0,2,1:T(8,128)}, u32[]{:S(2)}) copy-start(f32[128,160,32]{0,2,1:T(8,128)} %param.7) | copy-start | bytes 7864324
Sparse Core Ops, SparseCore 0:
  11.2 228.4 all-gather.1
where the time goes:
time: 336 us; the launch traced here: 335 us
  waiting for transfers between devices  229 us (68%)
  matrix products  72.3 us (22%)
  between operations  14.2 us (4%)
  blocking collectives  9.47 us (3%)
  local copies, waits for them, and re-layouts  8.13 us (2%)
    all_gather x1, waiting for transfers between devices, local(): gathered = lax.all_gather(kernel, 'vs', axis=3, tiled=True)  229 us
    dot_general x1, matrix products, complex_apply(): jnp.einsum(form, kern[:, 0], model[:, 1], preferred_element_type=jnp.floa...  9.96 us
    dot_general x1, matrix products, complex_apply(): jnp.einsum(form, kern[:, 1], model[:, 0], preferred_element_type=jnp.floa...  8.64 us
    dot_general x1, matrix products, complex_apply(): jnp.einsum(form, kern[:, 1], model[:, 1], preferred_element_type=jnp.floa...  8.64 us
    dot_general x1, matrix products, complex_apply(): jnp.einsum(form, kern[:, 0], model[:, 0], preferred_element_type=jnp.floa...  8.62 us
    unnamed x9, local copies, waits for them, and re-layouts  7.7 us
    dot_general x1, matrix products, complex_adjoint(): jnp.einsum(form, spectrum[:, 0], kern[:, 1], preferred_element_type=jnp.f...  7.33 us
    dot_general x1, matrix products, complex_adjoint(): jnp.einsum(form, spectrum[:, 1], kern[:, 1], preferred_element_type=jnp.f...  7.33 us
  transfers between devices with their start and end apart: 1, of which 1 were waited for; matrix products, arithmetic and copies ran while one was open for 0% of the time, Pallas kernels for 0%

commit v1 on v0

--- a/solution.py
+++ b/solution.py
@@ -5,6 +5,12 @@
 
 NS = 16384
 RW = 256
+
+
+def meet_the_regions(array_axis, mat):
+    state_next = lax.axis_size("vs")
+    left_arr = jnp.concatenate(state_next * [mat], axis=array_axis)
+    return lax.all_to_all(left_arr, "vs", array_axis, array_axis, tiled=True)
 
 
 def complex_apply(kern, model):
@@ -39,7 +45,7 @@
 
 
 def local(kernel, sources, observed, gate_start, gate_length):
-    gathered = lax.all_gather(kernel, "vs", axis=3, tiled=True)
+    gathered = meet_the_regions(3, kernel)
     forward = complex_apply(gathered, sources)
     field = forward.astype(jnp.bfloat16)
     timed = lax.all_to_all(field, "freq", split_axis=2, concat_axis=0, tiled=True)

time: 336 us -> 959 us (2.85)
  the two profiles are of different devices: /device:TPU:1 before, /device:TPU:99 now
where the time goes in v1:
time: 959 us; the launch traced here: 948 us
  waiting for transfers between devices  645 us (67%)
  local copies, waits for them, and re-layouts  203 us (21%)
  matrix products  76.4 us (8%)
  starting transfers between devices  10.1 us (1%)
    all_to_all x1, waiting for transfers between devices, meet_the_regions(): return lax.all_to_all(left_arr, 'vs', array_axis, array_axis, tiled=True)  645 us
    unnamed x88, local copies, waits for them, and re-layouts  176 us
    slice x1, local copies, waits for them, and re-layouts, complex_apply(): kern[:, 1]  26.1 us
  transfers between devices with their start and end apart: 1, of which 1 were waited for; matrix products, arithmetic and copies ran while one was open for 0% of the time, Pallas kernels for 0%

profile of v1, /device:TPU:99, one launch (start us, length us, event | category | flops | bytes accessed | tf_op | source)
XLA Modules:
  0.0 947.8 jit_solution(7560903681050962613)
XLA Ops:
  0.6 1.4 copy.78
  3.2 1.2 constant_dynamic-update-slice_fusion.62
  4.3 1.2 constant_dynamic-update-slice_fusion.61
  6.6 1.2 constant_dynamic-update-slice_fusion.59
  9.0 1.2 constant_dynamic-update-slice_fusion.57
  12.5 1.2 constant_dynamic-update-slice_fusion.54
  16.0 1.2 constant_dynamic-update-slice_fusion.51
  19.5 1.2 constant_dynamic-update-slice_fusion.48
  23.0 1.2 constant_dynamic-update-slice_fusion.45
  24.1 1.2 constant_dynamic-update-slice_fusion.44
  27.6 1.2 constant_dynamic-update-slice_fusion.41
  32.3 1.2 constant_dynamic-update-slice_fusion.37
  36.9 1.2 constant_dynamic-update-slice_fusion.33
  38.1 1.4 constant_dynamic-update-slice_fusion.32
  40.7 1.2 constant_dynamic-update-slice_fusion.30
  44.1 1.2 constant_dynamic-update-slice_fusion.27
  46.5 1.2 constant_dynamic-update-slice_fusion.25
  50.0 1.2 constant_dynamic-update-slice_fusion.22
  53.5 1.2 constant_dynamic-update-slice_fusion.19
  57.0 1.2 constant_dynamic-update-slice_fusion.16
  60.5 1.2 constant_dynamic-update-slice_fusion.13
  61.6 1.2 constant_dynamic-update-slice_fusion.12
  65.1 1.2 constant_dynamic-update-slice_fusion.9
  68.6 1.2 constant_dynamic-update-slice_fusion.6
  69.8 1.2 constant_dynamic-update-slice_fusion.5
  74.4 13.7 %constant_dynamic-update-slice_fusion.1 = bf16[2,2,256,16384]{2,0,1,3:T(2,128)(2,1)} fusion(bf16[2,2,256,16384]{2,0,1,3:T(2,128)(2,1)} %constant_dynamic-update-slice_fusion.2, bf16[2,2,256,256]{2,0,1,3:T(2,128)(2,1)S(1)} %copy.78), kind=kLoop, calls=%fused_computation.43 | loop fusion | bytes 1048576
  89.3 10.1 %all-to-all-start = ((bf16[2,2,256,16384]{2,0,1,3:T(2,128)(2,1)}), bf16[2,2,256,16384]{2,0,1,3:T(2,128)(2,1)}, u32[]{:S(2)}, u32[]{:S(2)}) async-start(bf16[2,2,256,16384]{2,0,1,3:T(2,128)(2,1)} %constant_dynamic-update-slice_fusion), calls=%async_computation | async-start | bytes 67108864 | tf_op jit(solution)/shard_map/all_to_all | solution.py:13
  99.5 645.0 %all-to-all-done = bf16[2,2,256,16384]{2,0,1,3:T(2,128)(2,1)} async-done(((bf16[2,2,256,16384]{2,0,1,3:T(2,128)(2,1)}), bf16[2,2,256,16384]{2,0,1,3:T(2,128)(2,1)}, u32[]{:S(2)}, u32[]{:S(2)}) %all-to-all-start) | async-done | bytes 33554464 | tf_op jit(solution)/shard_map/all_to_all | solution.py:13
  744.6 26.1 %fusion.90 = (bf16[2,1,256,16384]{2,0,1,3:T(2,128)(2,1)}, bf16[2,1,256,16384]{2,0,1,3:T(2,128)(2,1)}) fusion(bf16[2,2,256,16384]{2,0,1,3:T(2,128)(2,1)} %all-to-all-done), kind=kLoop, calls=%fused_computation.144 | loop fusion | bytes 67108864 | tf_op jit(solution)/shard_map/slice | solution.py:20
  770.6 41.0 %copy.155 = bf16[2,1,256,16384]{3,2,0,1:T(8,128)(2,1)} copy(bf16[2,1,256,16384]{2,0,1,3:T(2,128)(2,1)} %get-tuple-element.6) | data formatting | bytes 33554432
  811.6 9.8 %fusion.6 = f32[2,256,32]{1,2,0:T(8,128)S(1)} fusion(bf16[2,1,256,16384]{3,2,0,1:T(8,128)(2,1)} %copy.155, bf16[2,2,32,16384]{3,2,1,0:T(8,128)(2,1)} %param.6), kind=kOutput, calls=%fused_computation.8 | convolution fusion | flops 536870912 | bytes 18939904 | tf_op jit(solution)/shard_map/frs,fvs->frv/dot_general | solution.py:20
  821.5 9.8 %fusion.4 = f32[2,256,32]{1,2,0:T(8,128)S(1)} fusion(bf16[2,1,256,16384]{3,2,0,1:T(8,128)(2,1)} %copy.155, bf16[2,2,32,16384]{3,2,1,0:T(8,128)(2,1)} %param.6), kind=kOutput, calls=%fused_computation.6 | convolution fusion | flops 536870912 | bytes 18939904 | tf_op jit(solution)/shard_map/frs,fvs->frv/dot_general | solution.py:23
  831.3 41.1 %copy.153 = bf16[2,1,256,16384]{3,2,0,1:T(8,128)(2,1)} copy(bf16[2,1,256,16384]{2,0,1,3:T(2,128)(2,1)} %get-tuple-element.7) | data formatting | bytes 33554432
  872.4 8.9 fusion.50
  881.4 8.9 fusion.55
  890.8 5.3 all_to_all.41
  896.4 1.3 fusion.62
  897.8 2.9 fusion.17
  900.7 1.4 fusion.49
  902.2 1.4 fusion.48
  903.7 4.0 all_to_all.42
  907.8 8.9 fusion.10
  916.7 8.9 fusion.8
  925.6 3.0 copy.152
  928.7 10.9 %fusion = f32[2,1,32,16384]{3,2,0,1:T(8,128)} fusion(f32[2,32,16384]{2,1,0:T(8,128)S(1)} %fusion.10, bf16[2,1,256,16384]{3,2,0,1:T(8,128)(2,1)} %copy.155, bf16[2,2,256,32]{2,3,0,1:T(8,128)(2,1)S(1)} %all_to_all.37), kind=kOutput, calls=%fused_computation.2 | convolution fusion | flops 537919488 | bytes 25198592 | tf_op jit(solution)/shard_map/frv,frs->fvs/dot_general | solution.py:31
  939.6 3.0 fusion.1
  942.6 2.5 fusion.16
  945.1 2.3 copy.151
  (70 shorter events, 46.1 us)
Async XLA Ops:
  89.3 10.1 %copy-start.3 = (s32[128]{0:T(128)S(1)}, s32[128]{0:T(128)}, u32[]{:S(2)}) copy-start(s32[128]{0:T(128)} %param.8) | copy-start | bytes 1540
  89.3 10.1 %copy-start.4 = (s32[128]{0:T(128)S(1)}, s32[128]{0:T(128)}, u32[]{:S(2)}) copy-start(s32[128]{0:T(128)} %param.9) | copy-start | bytes 1540
  89.3 655.2 %all-to-all-start = ((bf16[2,2,256,16384]{2,0,1,3:T(2,128)(2,1)}), bf16[2,2,256,16384]{2,0,1,3:T(2,128)(2,1)}, u32[]{:S(2)}, u32[]{:S(2)}) async-start(bf16[2,2,256,16384]{2,0,1,3:T(2,128)(2,1)} %constant_dynamic-update-slice_fusion), calls=%async_computation | async-start | bytes 67108864 | tf_op jit(solution)/shard_map/all_to_all | solution.py:13
  831.3 66.5 %copy-start.2 = (f32[128,160,32]{0,2,1:T(8,128)S(1)}, f32[128,160,32]{0,2,1:T(8,128)}, u32[]{:S(2)}) copy-start(f32[128,160,32]{0,2,1:T(8,128)} %param.7) | copy-start | bytes 7864324
  900.7 1.5 copy-start
  907.8 17.8 %copy-start.1 = (f32[128,160,32]{0,1,2:T(8,128)S(1)}, f32[128,160,32]{0,1,2:T(8,128)}, u32[]{:S(2)}) copy-start(f32[128,160,32]{0,1,2:T(8,128)} %copy-done) | copy-start | bytes 7864324
  916.7 22.9 %slice-start = ((s8[16777216]{0:T(1024)(128)(4,1)}), s8[4194304]{0:T(1024)(128)(4,1)S(1)}, s32[]{:S(2)}) async-start(s8[16777216]{0:T(1024)(128)(4,1)} %bitcast.110), calls=%async_computation.3 | async-start | bytes 8388608
  916.7 22.9 %slice-start.1 = ((s8[16777216]{0:T(1024)(128)(4,1)}), s8[4194304]{0:T(1024)(128)(4,1)S(1)}, s32[]{:S(2)}) async-start(s8[16777216]{0:T(1024)(128)(4,1)} %bitcast.110), calls=%async_computation.4 | async-start | bytes 8388608
  925.6 14.0 %slice-start.2 = ((s8[16777216]{0:T(1024)(128)(4,1)}), s8[4194304]{0:T(1024)(128)(4,1)S(1)}, s32[]{:S(2)}) async-start(s8[16777216]{0:T(1024)(128)(4,1)} %bitcast.110), calls=%async_computation.5 | async-start | bytes 8388608
  928.7 10.9 %slice-start.3 = ((s8[16777216]{0:T(1024)(128)(4,1)}), s8[4194304]{0:T(1024)(128)(4,1)S(1)}, s32[]{:S(2)}) async-start(s8[16777216]{0:T(1024)(128)(4,1)} %bitcast.110), calls=%async_computation.6 | async-start | bytes 8388608
